TPU v7x, 128 devices: a whole 4x4x4 slice. The times are simulated.
128 devices in a mesh: dom: 16 (over x, y), tool: 8 (over z, core).
Axes of the slice: x: 4, y: 4, z: 4, core: 2. Of those that a mesh axis runs over, the one named last changes fastest.
Arguments:
- records: float32 [8192, 512], P(('dom', 'tool')), may hold values from -6 to 6
- tool_data: float32 [32768, 512], P(('dom', 'tool')), may hold values from -6 to 6
- owners: int32 [8192, 2], P(('dom', 'tool')), may hold values from 0 to 127, all different within a row; in each aligned block of 64 rows (0 to 63, 64 to 127, ...) at most 2 rows name the same one
- local_seg: int32 [8192, 2], P(('dom', 'tool')), may hold values from 0 to 255
- active: int32 [8192, 64], P(('dom', 'tool')), may hold values 0 or 1
- stiffness: float32 [8192, 5, 4096], P(('dom', 'tool')), may hold values from -0.3125 to 0.3125
- columns: int32 [8192, 5], P(('dom', 'tool')), may hold values from 0 to 67, as said below
- vectors: float32 [8192, 4096], P(('dom', 'tool')), may hold values from -6 to 6
Outputs:
- product: float32 [8192, 4096], P(('dom', 'tool'))
Inputs may be any that keep to these rules, and one draw needn't show every extreme that they name: Among the 64 node blocks of one device no owner is named by more than 2 candidates, a bound that some block reaches; a block's candidates name different owners. `columns`: the first column of each row is the row's own block, column 2 + b mod 64; the others lie within 2 blocks of it.
All inputs are finite; a program needn't handle non-finite values. No bound on the sum of `active` on one device may be relied on, other than what follows from the above.
Results may differ from a plain program's by a relative error of at most 0.0003.
Values sent between devices are 32-bit elements; how exact they have to be, the bound alone decides.
A program may use at most 128 MiB of HBM per device.

v0:
```python
import math
import jax
import jax.numpy as jnp
import numpy as np
from jax import lax
from jax.experimental import pallas as pl
from jax.experimental.pallas import tpu as pltpu
from jax.sharding import PartitionSpec as P
F32, BF16 = jnp.float32, jnp.bfloat16
NB, HB, E5 = 64, 2, 5
ALPHA = math.sqrt(math.log2(math.e) / 8.0)
TURN = 1.0 / (2.0 * math.pi)
def fit():
    r = np.cos(np.linspace(0, np.pi / 2, 4001))[:-1] * 0.5
    n = 6
    w = np.sqrt(2.0) * np.sin(np.pi * r) / r
    A = np.stack([r ** (2 * k) for k in range(n)], 1)
    c = np.linalg.lstsq(A * r[:, None], w * r, rcond=None)[0]
    return [float(x) for x in c], np.abs((A @ c - w) * r).max()
SINC, SERR = fit()

def split(x):
    hi = x.astype(BF16)
    return hi, (x - hi.astype(F32)).astype(BF16)

def to_w(src, dst, row0):
    for t in range(32):
        dst[pl.ds(row0 + t, 8, stride=32), :] = src[:, t * 128:(t + 1) * 128]

def prep_vec(vw, nat, bv, vt, c, own):
    lane = lax.broadcasted_iota(jnp.int32, (32, 128), 1)
    w = vw[pl.ds(pl.multiple_of(c * 32, 32), 32), :]
    wr = pltpu.roll(w, 64, 1)
    nat[pl.ds(0, 32, stride=2), :] = jnp.where(lane < 64, w, wr)
    nat[pl.ds(1, 32, stride=2), :] = jnp.where(lane < 64, wr, w)
    d = nat[...]
    lane2 = lax.broadcasted_iota(jnp.int32, (64, 128), 1)
    th, tl = split(jnp.where(lane2 < 64, d, 0.0))
    bh, bl = split(jnp.where(lane2 >= 64, d, 0.0))
    bv[c] = jnp.concatenate([jnp.concatenate([th, tl], 1), jnp.concatenate([bh, bl], 1)], 0)
    if own:
        vp = jnp.concatenate([w[:, :64], w[:, 64:]], 0)
        t = vp.T
        h, l = split(t)
        vt[c - HB] = jnp.concatenate([h, l], 0)

def prep_part(rec, act, rt, pb):
    rt[0:512, 0:64] = rec[...].T
    rt[512:576, 0:64] = act[...].astype(F32).T
    scale = (ALPHA,) * 3 + (3.0 * TURN,) * 3 + (TURN, 1.0, 1.0)
    def group(g, carry):
        for f in range(9):
            x = jnp.concatenate([rt[pl.ds(f * 64, 32, stride=2), :], rt[pl.ds(f * 64 + 1, 32, stride=2), :]], 0) * scale[f]
            x = pltpu.roll(x, 128 - g * 8, 1)
            for k in range(8):
                pb[g * 8 + k, f] = jnp.broadcast_to(x[:, k:k + 1], (64, 128))
        return carry
    lax.fori_loop(0, 8, group, 0)

def inner_block(cols, sw, bv, iw, b, bb):
    w = jnp.concatenate([sw[e, bb * 32:(bb + 1) * 32, :] for e in range(E5)], 1)
    h, l = split(w)
    r = jnp.concatenate([bv[cols[e, b]] for e in range(E5)], 0)
    o = jnp.dot(jnp.concatenate([h, l], 0), r, preferred_element_type=F32)
    iw[pl.ds(pl.multiple_of(b * 32, 32), 32), :] = (o[:32, :128] + o[:32, 128:]) + (o[32:, :128] + o[32:, 128:])

def cand_rows(got, s):
    x = got[s // 2]
    return jnp.where(lax.rem(s, 2) == 1, x[4:8], x[0:4])

def contact_block(slot, got, pb, vt, b):
    lane = lax.broadcasted_iota(jnp.int32, (4, 128), 1)
    sub = lax.broadcasted_iota(jnp.int32, (4, 128), 0)
    g0, g1 = cand_rows(got, slot[0, b]), cand_rows(got, slot[0, 64 + b])
    ev = jnp.where(lane < 64, g0, pltpu.roll(g1, 64, 1)) * jnp.where(sub < 2, ALPHA, 1.0)
    od = jnp.where(lane < 64, pltpu.roll(g0, 64, 1), g1) * jnp.where(sub < 1, ALPHA, 1.0)
    q = (ev[0:1], od[0:1], ev[1:2])
    m = (od[1:2], ev[2:3], od[2:3])
    thick, fric = ev[3:4], od[3:4]
    dist = sum((pb[b, f] - q[f]) ** 2 for f in range(3))
    x = sum(pb[b, 3 + f] * m[f] for f in range(3)) + pb[b, 6] * thick
    r = x - jnp.round(x)
    r2 = r * r
    s = SINC[5]
    for c in SINC[4::-1]:
        s = s * r2 + c
    s = s * r
    tile = jnp.exp2(-dist) * (1.0 - s * s) * ((jnp.tanh(pb[b, 7] * fric) * 0.5 + 1.0) * pb[b, 8])
    th, tl = split(tile)
    y = jnp.dot(vt[b], jnp.concatenate([th, tl], 1), preferred_element_type=F32)
    inw = (y[:64, :128] + y[:64, 128:]) + (y[64:, :128] + y[64:, 128:])
    ih, il = split(inw)
    o = lax.dot_general(jnp.concatenate([th, tl], 0), jnp.concatenate([ih, il], 0), (((1,), (1,)), ((), ())), preferred_element_type=F32)
    a = o[:64] + o[64:]
    ae, ao = a[:32], a[32:]
    l2 = lax.broadcasted_iota(jnp.int32, (32, 128), 1)
    return jnp.where(l2 < 64, ae, ao) + pltpu.roll(jnp.where(l2 < 64, ao, ae), 64, 1)

MESH = pl.DeviceIdType.MESH
N = 128


def peer(j):
    me = lax.axis_index("dom") * 8 + lax.axis_index("tool")
    d = lax.rem(me + j, N)
    return d, (d // 8, lax.rem(d, 8)), me


def exchange(own_ref, seg_ref, tool_ref, vec, got, slot_ref, lo, hi, req_s, req_r, resp, ss1, rs1, ss2, rs2, hs, hr):
    barrier = pltpu.get_barrier_semaphore()

    def sig(j, c):
        d, where, me = peer(j)
        pl.semaphore_signal(barrier, inc=1, device_id=where, device_id_type=MESH)
        return c

    lax.fori_loop(1, N, sig, 0)
    own = jnp.concatenate([own_ref[0:1, :], own_ref[1:2, :]], axis=1)
    seg = jnp.concatenate([seg_ref[0:1, :], seg_ref[1:2, :]], axis=1)
    row = lax.broadcasted_iota(jnp.int32, (N, N), 0)
    col = lax.broadcasted_iota(jnp.int32, (N, N), 1)
    hit = jnp.broadcast_to(own, (N, N)) == row
    key = jnp.broadcast_to(col[0:1] * 256 + seg, (N, N))
    kmin = jnp.min(jnp.where(hit, key, 1 << 20), axis=1, keepdims=True)
    kmax = jnp.max(jnp.where(hit, key, 0), axis=1, keepdims=True)
    req_s[...] = (jnp.where(col == 0, kmin, kmax) & 255).reshape(N, 1, N)
    slot_ref[...] = own * 2 + jnp.sum(jnp.where(hit & (key != kmin), 1, 0), axis=0, keepdims=True)
    pl.semaphore_wait(barrier, N - 1)
    me = lax.axis_index("dom") * 8 + lax.axis_index("tool")
    nxt, after, _ = peer(1)
    prv, before, _ = peer(N - 1)
    down = pltpu.make_async_remote_copy(vec.at[pl.ds(56, 8)], lo, hs.at[0], hr.at[0], device_id=after, device_id_type=MESH)
    up = pltpu.make_async_remote_copy(vec.at[pl.ds(0, 8)], hi, hs.at[1], hr.at[1], device_id=before, device_id_type=MESH)
    pltpu.make_async_copy(req_s.at[me], req_r.at[me], rs1).start()

    def send(j, c):
        d, where, me = peer(j)
        pltpu.make_async_remote_copy(req_s.at[d], req_r.at[me], ss1, rs1, device_id=where, device_id_type=MESH).start()
        return c

    lax.fori_loop(1, N, send, 0)
    down.start()
    up.start()
    pltpu.make_async_copy(req_r, req_r, rs1).wait()
    ask = req_r[...].reshape(N, N)
    for r in range(2):
        hot = (lax.broadcasted_iota(jnp.int32, (N, 256), 1) == ask[:, r:r + 1]).astype(jnp.float32)
        g = jnp.dot(hot, tool_ref[...], precision=lax.Precision.HIGHEST, preferred_element_type=jnp.float32)
        for f in range(4):
            resp[:, r * 4 + f, :] = g[:, f * 128:(f + 1) * 128]
    pltpu.make_async_copy(req_s.at[pl.ds(0, N - 1)], req_s.at[pl.ds(0, N - 1)], ss1).wait()
    pltpu.make_async_copy(resp.at[me], got.at[me], rs2).start()

    def reply(j, c):
        d, where, me = peer(j)
        pltpu.make_async_remote_copy(resp.at[d], got.at[me], ss2, rs2, device_id=where, device_id_type=MESH).start()
        return c

    lax.fori_loop(1, N, reply, 0)
    down.wait()
    up.wait()

    @pl.when(me == 0)
    def _():
        lo[...] = jnp.zeros_like(lo)

    @pl.when(me == N - 1)
    def _():
        hi[...] = jnp.zeros_like(hi)

    pltpu.make_async_copy(got, got, rs2).wait()
    pltpu.make_async_copy(resp.at[pl.ds(0, N - 1)], resp.at[pl.ds(0, N - 1)], ss2).wait()

def body(slot, cols, got, rec, act, s_hbm, vec, lo, hi, out, s_v, sw, vw, nat, bv, vt, rt, pb, iw, sems):
    def cp(g): return pltpu.make_async_copy(s_hbm.at[:, pl.ds(pl.multiple_of(g*8,8),8), :], s_v.at[:, pl.ds(pl.multiple_of(g*8,8),8), :], sems.at[g])
    for g in range(8): cp(g).start()
    to_w(lo, vw, 0); to_w(hi, vw, 256+2048)
    def tw(g, c):
        to_w(vec[pl.ds(pl.multiple_of(g*8,8),8),:], vw, 256+g*256); return c
    lax.fori_loop(0,8,tw,0)
    vww = vw.at[pl.ds(192, 68*32)]
    for c in (0,1,66,67): prep_vec(vww, nat, bv, vt, c, False)
    def pv(c, k): prep_vec(vww, nat, bv, vt, c, True); return k
    lax.fori_loop(2,66,pv,0)
    prep_part(rec, act, rt, pb)
    def ig(g, c):
        cp(g).wait()
        for e in range(E5): to_w(s_v[e, pl.ds(pl.multiple_of(g*8,8),8), :], sw.at[e], 0)
        for bb in range(8): inner_block(cols, sw, bv, iw, g*8+bb, bb)
        return c
    lax.fori_loop(0,8,ig,0)
    def cg(b, c):
        z = contact_block(slot, got, pb, vt, b)
        iw[pl.ds(pl.multiple_of(b*32,32),32),:] = iw[pl.ds(pl.multiple_of(b*32,32),32),:] + 0.05*z
        return c
    lax.fori_loop(0,64,cg,0)
    def og(g, c):
        for t in range(32):
            out[pl.ds(pl.multiple_of(g*8,8),8), t*128:(t+1)*128] = iw[pl.ds(g*256+t, 8, stride=32), :]
        return c
    lax.fori_loop(0,8,og,0)

V = pl.BlockSpec(memory_space=pltpu.VMEM)
S = pl.BlockSpec(memory_space=pltpu.SMEM)
A = pl.BlockSpec(memory_space=pl.ANY)


def per_device(records, tool_data, owners, local_seg, active, stiffness, columns, vectors):
    got, slot, lo, hi = pl.pallas_call(
        exchange,
        out_shape=(jax.ShapeDtypeStruct((N, 8, 128), F32), jax.ShapeDtypeStruct((1, N), jnp.int32),
                   jax.ShapeDtypeStruct((8, 4096), F32), jax.ShapeDtypeStruct((8, 4096), F32)),
        in_specs=[V, V, V, A], out_specs=(V, V, V, V),
        scratch_shapes=[pltpu.VMEM((N, 1, N), jnp.int32), pltpu.VMEM((N, 1, N), jnp.int32), pltpu.VMEM((N, 8, 128), F32)]
        + [pltpu.SemaphoreType.DMA] * 4 + [pltpu.SemaphoreType.DMA((2,))] * 2,
        compiler_params=pltpu.CompilerParams(collective_id=0, has_side_effects=True, vmem_limit_bytes=40 << 20),
        name="exchange",
    )(owners.T, local_seg.T, tool_data, vectors)
    return pl.pallas_call(
        body, out_shape=jax.ShapeDtypeStruct((NB, 4096), F32),
        in_specs=[S, S, V, V, V, A, V, V, V], out_specs=V,
        scratch_shapes=[pltpu.VMEM((5, 64, 4096), F32), pltpu.VMEM((5, 256, 128), F32), pltpu.VMEM((80 * 32, 128), F32),
                        pltpu.VMEM((64, 128), F32), pltpu.VMEM((68, 128, 256), BF16), pltpu.VMEM((64, 128, 64), BF16),
                        pltpu.VMEM((576, 128), F32), pltpu.VMEM((64, 9, 64, 128), F32), pltpu.VMEM((2048, 128), F32),
                        pltpu.SemaphoreType.DMA((8,))],
        compiler_params=pltpu.CompilerParams(vmem_limit_bytes=60 << 20), name="mortar",
    )(slot, columns.T, got, records, active, stiffness.transpose(1, 0, 2), vectors, lo, hi)


def solution(mesh):
    ax = P(("dom", "tool"), None)
    return jax.shard_map(per_device, mesh=mesh, in_specs=(ax,) * 5 + (P(("dom", "tool"), None, None), ax, ax), out_specs=ax, check_vma=False)
```

profile of v0, /device:TPU:1, one launch (start us, length us, event | category | flops | bytes accessed | tf_op | source)
XLA Modules:
  0.0 104.5 jit_solution(4148706331319066182)
XLA Ops:
  0.0 0.0 copy-start
  0.0 1.2 %copy-done = f32[64,4096]{1,0:T(8,128)S(1)} copy-done((f32[64,4096]{1,0:T(8,128)S(1)}, f32[64,4096]{1,0:T(8,128)}, u32[]{:S(2)}) %copy-start) | copy-done | bytes 1048600
  1.2 0.0 copy-start.1
  1.2 1.0 copy-done.1
  2.3 0.0 copy-start.5
  2.3 0.7 copy-done.5
  2.9 0.0 copy-start.6
  2.9 0.7 copy-done.6
  3.6 30.0 %exchange.1 = (f32[128,8,128]{2,1,0:T(8,128)S(1)}, s32[1,128]{1,0:T(1,128)S(1)}, f32[8,4096]{1,0:T(8,128)S(1)}, f32[8,4096]{1,0:T(8,128)S(1)}) custom-call(s32[2,64]{1,0:T(2,128)S(1)} %bitcast.4, s32[2,64]{1,0:T(2,128)S(1)} %bitcast.5, f32[256,512]{1,0:T(8,128)S(1)} %copy-done.1, f32[64,4096]{1,0:T(8,128)S(1)} %copy-done), custom_call_target="tpu_custom_call" | custom-call | tf_op jit(solution)/shard_map/exchange/pallas_call | solution.py:209
  33.6 0.0 copy-start.2
  33.6 0.8 copy-done.2
  34.4 0.0 copy-start.3
  34.4 0.7 copy-done.3
  35.1 0.0 copy-start.4
  35.1 0.7 copy-done.4
  35.7 0.0 copy-start.7
  35.7 0.6 copy-done.7
  36.3 68.2 %mortar.1 = f32[64,4096]{1,0:T(8,128)} custom-call(s32[1,128]{1,0:T(1,128)} %copy-done.7, s32[5,64]{1,0:T(8,128)} %bitcast.7, f32[128,8,128]{2,1,0:T(8,128)} %copy-done.2, f32[64,512]{1,0:T(8,128)} %rec.1, s32[64,64]{1,0:T(8,128)} %act.1, f32[5,64,4096]{2,1,0:T(8,128)} %bitcast.6, f32[64,4096]{1,0:T(8,128)} %vec.3, f32[8,4096]{1,0:T(8,128)} %copy-done.3, ...), custom_call_target="tpu_custom_call" | custom-call | tf_op jit(solution)/shard_map/mortar/pallas_call | solution.py:219
Async XLA Ops:
  0.0 1.2 %copy-start = (f32[64,4096]{1,0:T(8,128)S(1)}, f32[64,4096]{1,0:T(8,128)}, u32[]{:S(2)}) copy-start(f32[64,4096]{1,0:T(8,128)} %vec.3) | copy-start | bytes 3145732
  1.2 1.0 copy-start.1
  2.3 0.7 copy-start.5
  2.9 0.7 copy-start.6
  33.6 0.8 copy-start.2
  34.4 0.7 copy-start.3
  35.1 0.7 copy-start.4
  35.7 0.6 copy-start.7
where the time goes:
time: 105 us; the launch traced here: 104 us
  Pallas kernels  98.2 us (94%)
  local copies, waits for them, and re-layouts  6.31 us (6%)
    pallas_call x1, Pallas kernels, per_device(): pl.pallas_call(body, out_shape=jax.ShapeDtypeStruct((NB, 4096), F32), in_...  68.2 us
    pallas_call x1, Pallas kernels, per_device(): pl.pallas_call(exchange, out_shape=(jax.ShapeDtypeStruct((N, 8, 128), F32...  30 us
    unnamed x16, local copies, waits for them, and re-layouts  6.31 us

commit v1 on v0

v1 whole, which is shorter than its diff:
```python
import math
import jax
import jax.numpy as jnp
import numpy as np
from jax import lax
from jax.experimental import pallas as pl
from jax.experimental.pallas import tpu as pltpu
from jax.sharding import PartitionSpec as P
F32, BF16 = jnp.float32, jnp.bfloat16
NB, HB, E5 = 64, 2, 5
A2 = math.log2(math.e) / 8.0
TURN = 1.0 / (2.0 * math.pi)
def fit():
    r = np.cos(np.linspace(0, np.pi / 2, 4001))[:-1] * 0.5
    w = np.sqrt(2.0) * np.sin(np.pi * r) / r
    a = np.stack([r ** (2 * k) for k in range(5)], 1)
    c = np.linalg.lstsq(a * r[:, None], w * r, rcond=None)[0]
    return [float(x) for x in c]


SINC = fit()

def iota(shape, dim):
    return lax.broadcasted_iota(jnp.int32, shape, dim)

def split(x):
    hi = x.astype(BF16)
    return hi, (x - hi.astype(F32)).astype(BF16)

def split3(x):
    h = x.astype(BF16).astype(F32)
    y = x - h
    m = y.astype(BF16).astype(F32)
    return h, m, y - m

def to_w(src, dst, row0):
    for t in range(32):
        dst[pl.ds(row0 + t, 8, stride=32), :] = src[:, t * 128:(t + 1) * 128]

def pair8(g0, g1):
    lane = iota((4, 128), 1)
    ev = jnp.where(lane < 64, g0, pltpu.roll(g1, 64, 1))
    od = jnp.where(lane < 64, pltpu.roll(g0, 64, 1), g1)
    return jnp.concatenate([ev, od], 0)

def mask_rows(which):
    s = iota((8, 128), 0)
    m = s == which[0]
    for w in which[1:]:
        m = m | (s == w)
    return m

def square_sum(x):
    return jnp.sum(jnp.where(mask_rows((0, 1, 4)), x * x, 0.0), 0, keepdims=True) * A2

def prep_vec(vw, nat, bv, c, own_b, vt, dw):
    w = vw[pl.ds(pl.multiple_of(c * 32, 32), 32), :]
    lane = iota((32, 128), 1)
    wr = pltpu.roll(w, 64, 1)
    nat[pl.ds(0, 32, stride=2), :] = jnp.where(lane < 64, w, wr)
    nat[pl.ds(1, 32, stride=2), :] = jnp.where(lane < 64, wr, w)
    d = nat[...]
    lane2 = iota((64, 128), 1)
    h, l = split(d)
    z = jnp.zeros_like(h)
    lo, up = lane2 < 64, lane2 >= 64
    bv[c] = jnp.concatenate([jnp.concatenate([jnp.where(lo, h, z), jnp.where(lo, l, z)], 1),
                             jnp.concatenate([jnp.where(up, h, z), jnp.where(up, l, z)], 1)], 0)
    if own_b is not None:
        w = w * dw[own_b]
        t = jnp.concatenate([w[:, :64], w[:, 64:]], 0).T
        h, l = split(t)
        vt[own_b] = jnp.concatenate([h, h, l], 1)

def prep_act(act, at, dw):
    at[...] = act[...].astype(F32).T
    a = jnp.concatenate([at[pl.ds(0, 32, stride=2), :], at[pl.ds(1, 32, stride=2), :]], 1).astype(BF16)
    row, col = iota((128, 128), 0), iota((128, 128), 1)
    same = (row // 64) == (col // 64)
    def one(g, carry):
        for k in range(4):
            b = g * 4 + k
            hot = jnp.where(same & (lax.rem(row, 64) == b), 1.0, 0.0).astype(BF16)
            dw[b] = jnp.dot(a, hot, preferred_element_type=F32)
        return carry
    lax.fori_loop(0, 16, one, 0)

def prep_part(rw, ft, lhs, g, k):
    r4 = rw[pl.ds(pl.multiple_of(g * 8, 8), 8), :]
    p = pair8(r4[0:4], r4[4:8])
    sub = iota((8, 128), 0)
    pos = mask_rows((0, 1, 4))
    ph, pm, pl_ = split3(-square_sum(p))
    extra = jnp.where(sub < 3, -1.0, jnp.where(sub == 3, ph, jnp.where(sub == 4, pm, jnp.where(sub == 5, pl_, 0.0))))
    scale = jnp.where(pos, 2.0 * A2, jnp.where(sub == 7, 1.0, jnp.where(sub == 3, TURN, 3.0 * TURN)))
    h, m, l = split3(p * scale)
    zero = jnp.zeros_like(h)
    for n, mk in enumerate((pos, mask_rows((2, 3, 5, 6)), sub == 7)):
        hh, mm, ll = (jnp.where(mk, x, 0.0) for x in (h, m, l))
        f = jnp.concatenate([hh, hh, hh, mm, mm, ll, extra if n == 0 else zero, zero], 0)
        ft[n, k] = f.T
    for q in range(2):
        parts = []
        for n in range(3):
            for par in range(2):
                parts.append(ft[n, k, pl.ds(q * 64 + par, 32, stride=2), :])
        lhs[g * 2 + q] = jnp.concatenate(parts, 0).astype(BF16)

def inner_block(cols, sw, bv, iw, b, bb):
    w = jnp.concatenate([sw[e, bb * 32:(bb + 1) * 32, :] for e in range(E5)], 1)
    h, l = split(w)
    r = jnp.concatenate([bv[cols[e, b]] for e in range(E5)], 0)
    o = jnp.dot(jnp.concatenate([h, l], 0), r, preferred_element_type=F32)
    iw[pl.ds(pl.multiple_of(b * 32, 32), 32), :] = (o[:32, :128] + o[:32, 128:]) + (o[32:, :128] + o[32:, 128:])

def cand_rows(got, s):
    x = got[s // 2]
    return jnp.where(lax.rem(s, 2) == 1, x[4:8], x[0:4])

def tile_of(slot, got, lhs, b):
    x = pair8(cand_rows(got, slot[0, b]), cand_rows(got, slot[0, 64 + b]))
    sub = iota((8, 128), 0)
    h, m, l = split3(x)
    qh, qm, ql = split3(square_sum(x))
    extra = jnp.where(sub == 0, qh, jnp.where(sub == 1, qm, jnp.where(sub == 2, ql, jnp.where(sub < 6, 1.0, 0.0))))
    rhs = jnp.concatenate([h, m, l, h, m, h, extra, jnp.zeros_like(h)], 0).astype(BF16)
    z = jnp.dot(lhs[b], rhs, preferred_element_type=F32)
    x = z[64:128]
    r = x - jnp.round(x)
    r2 = r * r
    s = SINC[4]
    for c in SINC[3::-1]:
        s = s * r2 + c
    s = s * r
    tile = jnp.exp2(z[:64]) * (1.0 - s * s) * (jnp.tanh(z[128:]) * 0.5 + 1.0)
    return split(tile)

def first(vt, b, th, tl):
    y = jnp.dot(vt[b], jnp.concatenate([th, tl, th], 0), preferred_element_type=F32)
    return split(y)

def second(dw, b, th, tl, ih, il):
    o = lax.dot_general(jnp.concatenate([th, th, tl], 1), jnp.concatenate([ih, il, ih], 1), (((1,), (1,)), ((), ())), preferred_element_type=F32)
    return jnp.concatenate([o[:32], o[32:]], 1) * (dw[b] * 0.05)

MESH = pl.DeviceIdType.MESH
N = 128
UC = 8


def peer(j):
    me = lax.axis_index("dom") * 8 + lax.axis_index("tool")
    d = lax.rem(me + j, N)
    return d, (d // 8, lax.rem(d, 8)), me


def rows8(g):
    return pl.ds(pl.multiple_of(g * 8, 8), 8)


def local(src, dst, sem):
    return pltpu.make_async_copy(src, dst, sem)


def kernel(own_h, seg_h, tool_h, vec_h, cols_h, rec_h, act_h, s_h, out,
           own_v, seg_v, tool, vec, cols, rec, act, s_v, slot_v, slot,
           req_s, req_r, resp, got, lo, hi,
           sw, vw, nat, bv, vt, at, dw, rw, ft, lhs, iw,
           ls, gs, ss1, rs1, ss2, rs2, hs, hr):
    loads = [local(a, b, ls.at[i]) for i, (a, b) in enumerate(
        ((own_h, own_v), (seg_h, seg_v), (tool_h, tool), (vec_h, vec), (cols_h, cols), (rec_h, rec), (act_h, act)))]
    for c in loads:
        c.start()

    def stiff(g):
        return local(s_h.at[:, rows8(g), :], s_v.at[:, rows8(g), :], gs.at[g])

    for g in range(8):
        stiff(g).start()
    barrier = pltpu.get_barrier_semaphore()

    def sig(j, c):
        d, where, me = peer(j)
        pl.semaphore_signal(barrier, inc=1, device_id=where, device_id_type=MESH)
        return c

    lax.fori_loop(1, N, sig, 0)
    loads[0].wait()
    loads[1].wait()
    own = jnp.concatenate([own_v[0:1, :], own_v[1:2, :]], axis=1)
    seg = jnp.concatenate([seg_v[0:1, :], seg_v[1:2, :]], axis=1)
    row, col = iota((N, N), 0), iota((N, N), 1)
    hit = jnp.broadcast_to(own, (N, N)) == row
    key = jnp.broadcast_to(col[0:1] * 256 + seg, (N, N))
    kmin = jnp.min(jnp.where(hit, key, 1 << 20), axis=1, keepdims=True)
    kmax = jnp.max(jnp.where(hit, key, 0), axis=1, keepdims=True)
    req_s[...] = (jnp.where(col == 0, kmin, kmax) & 255).reshape(N, 1, N)
    slot_v[...] = own * 2 + jnp.sum(jnp.where(hit & (key != kmin), 1, 0), axis=0, keepdims=True)
    pl.semaphore_wait(barrier, N - 1)
    me = lax.axis_index("dom") * 8 + lax.axis_index("tool")
    _, after, _ = peer(1)
    _, before, _ = peer(N - 1)
    down = pltpu.make_async_remote_copy(vec_h.at[pl.ds(56, 8)], lo, hs.at[0], hr.at[0], device_id=after, device_id_type=MESH)
    up = pltpu.make_async_remote_copy(vec_h.at[pl.ds(0, 8)], hi, hs.at[1], hr.at[1], device_id=before, device_id_type=MESH)
    local(req_s.at[me], req_r.at[me], rs1).start()

    def send(j, c):
        d, where, me = peer(j)
        pltpu.make_async_remote_copy(req_s.at[d], req_r.at[me], ss1, rs1, device_id=where, device_id_type=MESH).start()
        return c

    lax.fori_loop(1, N, send, 0)
    down.start()
    up.start()
    keep = local(slot_v, slot, ls.at[7])
    keep.start()
    loads[3].wait()
    loads[6].wait()
    prep_act(act, at, dw)
    vww = vw.at[pl.ds(192, 68 * 32)]

    def relay(g, c):
        to_w(vec[rows8(g), :], vw, 256 + g * 256)
        return c

    lax.fori_loop(0, 8, relay, 0)

    def pv(g, c):
        for u in range(4):
            prep_vec(vww, nat.at[u], bv, g * 4 + u + 2, g * 4 + u, vt, dw)
        return c

    lax.fori_loop(0, 16, pv, 0)
    loads[2].wait()
    local(req_r, req_r, rs1).wait()
    ask = req_r[...].reshape(N, N)
    for r in range(2):
        hot = (iota((N, 256), 1) == ask[:, r:r + 1]).astype(F32)
        g = jnp.dot(hot, tool[...], precision=lax.Precision.HIGHEST, preferred_element_type=F32)
        for f in range(4):
            resp[:, r * 4 + f, :] = g[:, f * 128:(f + 1) * 128]
    local(resp.at[me], got.at[me], rs2).start()

    def reply(j, c):
        d, where, me = peer(j)
        pltpu.make_async_remote_copy(resp.at[d], got.at[me], ss2, rs2, device_id=where, device_id_type=MESH).start()
        return c

    lax.fori_loop(1, N, reply, 0)
    down.wait()
    up.wait()

    @pl.when(me == 0)
    def _():
        lo[...] = jnp.zeros_like(lo)

    @pl.when(me == N - 1)
    def _():
        hi[...] = jnp.zeros_like(hi)

    to_w(lo, vw, 0)
    to_w(hi, vw, 256 + 2048)
    for i, c in enumerate((0, 1, 66, 67)):
        prep_vec(vww, nat.at[i], bv, c, None, vt, dw)
    loads[5].wait()
    for b0 in range(8):
        for f in range(4):
            rw[pl.ds(b0 * 32 + f, 8, stride=4), :] = rec[b0 * 8:b0 * 8 + 8, f * 128:(f + 1) * 128]

    def pp(g, c):
        for u in range(2):
            prep_part(rw, ft, lhs, g * 2 + u, u)
        return c

    lax.fori_loop(0, 16, pp, 0)
    loads[4].wait()

    def ig(g, c):
        stiff(g).wait()
        for e in range(E5):
            to_w(s_v[e, rows8(g), :], sw.at[e], 0)
        for bb in range(8):
            inner_block(cols, sw, bv, iw, g * 8 + bb, bb)
        return c

    lax.fori_loop(0, 8, ig, 0)
    keep.wait()
    local(req_s.at[pl.ds(0, N - 1)], req_s.at[pl.ds(0, N - 1)], ss1).wait()
    local(got, got, rs2).wait()

    def cg(g, c):
        bs = [g * UC + u for u in range(UC)]
        t = [tile_of(slot, got, lhs, b) for b in bs]
        y = [first(vt, b, *x) for b, x in zip(bs, t)]
        z = [second(dw, b, *x, *w) for b, x, w in zip(bs, t, y)]
        at32 = [pl.ds(pl.multiple_of(b * 32, 32), 32) for b in bs]
        total = [iw[a, :] + w for a, w in zip(at32, z)]
        for a, w in zip(at32, total):
            iw[a, :] = w
        return c

    lax.fori_loop(0, NB // UC, cg, 0)

    def og(g, c):
        for t in range(32):
            out[rows8(g), t * 128:(t + 1) * 128] = iw[pl.ds(g * 256 + t, 8, stride=32), :]
        return c

    lax.fori_loop(0, 8, og, 0)
    local(resp.at[pl.ds(0, N - 1)], resp.at[pl.ds(0, N - 1)], ss2).wait()


def per_device(records, tool_data, owners, local_seg, active, stiffness, columns, vectors):
    vm, sm, dma = pltpu.VMEM, pltpu.SMEM, pltpu.SemaphoreType.DMA
    i32 = jnp.int32
    return pl.pallas_call(
        kernel,
        out_shape=jax.ShapeDtypeStruct((NB, 4096), F32),
        in_specs=[pl.BlockSpec(memory_space=pl.ANY)] * 8,
        out_specs=pl.BlockSpec(memory_space=vm),
        scratch_shapes=[
            vm((2, NB), i32), vm((2, NB), i32), vm((256, 512), F32), vm((NB, 4096), F32), sm((E5, NB), i32),
            vm((NB, 512), F32), vm((NB, 64), i32), vm((E5, NB, 4096), F32), vm((1, N), i32), sm((1, N), i32),
            vm((N, 1, N), i32), vm((N, 1, N), i32), vm((N, 8, 128), F32), vm((N, 8, 128), F32),
            vm((8, 4096), F32), vm((8, 4096), F32),
            vm((E5, 256, 128), F32), vm((80 * 32, 128), F32), vm((4, 64, 128), F32), vm((68, 128, 256), BF16),
            vm((NB, 64, 192), BF16), vm((64, 64), F32), vm((NB, 32, 128), F32), vm((256, 128), F32),
            vm((3, 2, 128, 64), F32), vm((NB, 192, 64), BF16), vm((2048, 128), F32),
            dma((8,)), dma((8,)), dma, dma, dma, dma, dma((2,)), dma((2,)),
        ],
        compiler_params=pltpu.CompilerParams(collective_id=0, has_side_effects=True, vmem_limit_bytes=60 << 20),
        name="mortar",
    )(owners.T, local_seg.T, tool_data, vectors, columns.T, records, active, stiffness.transpose(1, 0, 2))


def solution(mesh):
    ax = P(("dom", "tool"), None)
    return jax.shard_map(per_device, mesh=mesh, in_specs=(ax,) * 5 + (P(("dom", "tool"), None, None), ax, ax), out_specs=ax, check_vma=False)
```

time: 105 us -> 48.4 us (0.46)
  Pallas kernels: 98.2 us -> 46 us
  local copies, waits for them, and re-layouts: 6.31 us -> 2.27 us
    pallas_call x2 -> x1, Pallas kernels: 98.2 us -> 46 us  [per_device(): pl.pallas_call(kernel, out_shape=jax.ShapeDtypeStruct((NB, 4096), F32), i...]
    unnamed x16 -> x1, local copies, waits for them, and re-layouts: 6.31 us -> 2.27 us
where the time goes in v1:
time: 48.4 us; the launch traced here: 48.2 us
  Pallas kernels  46 us (95%)
  local copies, waits for them, and re-layouts  2.27 us (5%)
    pallas_call x1, Pallas kernels, per_device(): pl.pallas_call(kernel, out_shape=jax.ShapeDtypeStruct((NB, 4096), F32), i...  46 us
    unnamed x1, local copies, waits for them, and re-layouts  2.27 us

profile of v1, /device:TPU:1, one launch (start us, length us, event | category | flops | bytes accessed | tf_op | source)
XLA Modules:
  0.0 48.2 jit_solution(10978904332065647889)
XLA Ops:
  0.0 46.0 %mortar.1 = f32[64,4096]{1,0:T(8,128)} custom-call(s32[2,64]{1,0:T(2,128)} %bitcast.6, s32[2,64]{1,0:T(2,128)} %bitcast.7, f32[256,512]{1,0:T(8,128)} %tool_h.1, f32[64,4096]{1,0:T(8,128)} %vec_h.1, s32[5,64]{1,0:T(8,128)} %bitcast.5, f32[64,512]{1,0:T(8,128)} %rec_h.1, s32[64,64]{1,0:T(8,128)} %act_h.1, f32[5,64,4096]{2,1,0:T(8,128)} %bitcast.4), custom_call_target="tpu_custom_call" | custom-call | tf_op jit(solution)/shard_map/mortar/pallas_call | solution.py:316
  46.0 2.3 %copy.10 = f32[64,4096]{1,0:T(8,128)} copy(f32[64,4096]{1,0:T(8,128)} %mortar.1) | data formatting | bytes 2097152

commit v2 on v1

--- a/solution.py
+++ b/solution.py
@@ -118,7 +118,7 @@
     return jnp.where(lax.rem(s, 2) == 1, x[4:8], x[0:4])
 
 def tile_of(slot, got, lhs, b):
-    x = pair8(cand_rows(got, slot[0, b]), cand_rows(got, slot[0, 64 + b]))
+    x = pair8(cand_rows(got, slot[0, b]), cand_rows(got, slot[0, NB + b]))
     sub = iota((8, 128), 0)
     h, m, l = split3(x)
     qh, qm, ql = split3(square_sum(x))
@@ -145,13 +145,7 @@
 
 MESH = pl.DeviceIdType.MESH
 N = 128
-UC = 8
-
-
-def peer(j):
-    me = lax.axis_index("dom") * 8 + lax.axis_index("tool")
-    d = lax.rem(me + j, N)
-    return d, (d // 8, lax.rem(d, 8)), me
+UC = 16
 
 
 def rows8(g):
@@ -162,13 +156,16 @@
     return pltpu.make_async_copy(src, dst, sem)
 
 
-def kernel(own_h, seg_h, tool_h, vec_h, cols_h, rec_h, act_h, s_h, out,
-           own_v, seg_v, tool, vec, cols, rec, act, s_v, slot_v, slot,
-           req_s, req_r, resp, got, lo, hi,
-           sw, vw, nat, bv, vt, at, dw, rw, ft, lhs, iw,
-           ls, gs, ss1, rs1, ss2, rs2, hs, hr):
+def remote(src, dst, send, recv, where):
+    return pltpu.make_async_remote_copy(src, dst, send, recv, device_id=where, device_id_type=MESH)
+
+
+def gather_kernel(own_h, seg_h, tool_h, vec_h, cols_h, rec_h, act_h, s_h, iw,
+                  own_v, seg_v, tool, vec, cols, rec, act, s_v, slot_v, slot,
+                  req_s, req_m, req_r, resp, got, lo, hi, sw, vw, nat, bv, vt, at, dw, rw, ft, lhs,
+                  ls, gs, ss1, rs1, ss2, rs2, ss3, rs3, hs, hr):
     loads = [local(a, b, ls.at[i]) for i, (a, b) in enumerate(
-        ((own_h, own_v), (seg_h, seg_v), (tool_h, tool), (vec_h, vec), (cols_h, cols), (rec_h, rec), (act_h, act)))]
+        ((own_h, own_v), (seg_h, seg_v), (act_h, act), (vec_h, vec), (rec_h, rec), (tool_h, tool), (cols_h, cols)))]
     for c in loads:
         c.start()
 
@@ -177,53 +174,48 @@
 
     for g in range(8):
         stiff(g).start()
+    dom, tl = lax.axis_index("dom"), lax.axis_index("tool")
+    me = dom * 8 + tl
+    px, py = dom // 4, lax.rem(dom, 4)
+    span = [(lax.rem(px + a, 4) * 4 + lax.rem(py + b, 4), tl)
+            for a, b in ((2, 2), (2, 1), (2, 3), (1, 2), (3, 2), (1, 1), (1, 3), (3, 1), (3, 3), (2, 0), (0, 2), (1, 0), (3, 0), (0, 1), (0, 3))]
+    part = [(dom, lax.rem(tl + j, 8)) for j in (4, 3, 5, 2, 6, 1, 7)]
+    nxt, prv = lax.rem(me + 1, N), lax.rem(me + N - 1, N)
+    after, before = (nxt // 8, lax.rem(nxt, 8)), (prv // 8, lax.rem(prv, 8))
     barrier = pltpu.get_barrier_semaphore()
-
-    def sig(j, c):
-        d, where, me = peer(j)
+    for where in span + part + [after, before]:
         pl.semaphore_signal(barrier, inc=1, device_id=where, device_id_type=MESH)
-        return c
-
-    lax.fori_loop(1, N, sig, 0)
     loads[0].wait()
     loads[1].wait()
     own = jnp.concatenate([own_v[0:1, :], own_v[1:2, :]], axis=1)
     seg = jnp.concatenate([seg_v[0:1, :], seg_v[1:2, :]], axis=1)
     row, col = iota((N, N), 0), iota((N, N), 1)
-    hit = jnp.broadcast_to(own, (N, N)) == row
+    hit = jnp.broadcast_to(lax.rem(own, 8) * 16 + own // 8, (N, N)) == row
     key = jnp.broadcast_to(col[0:1] * 256 + seg, (N, N))
     kmin = jnp.min(jnp.where(hit, key, 1 << 20), axis=1, keepdims=True)
     kmax = jnp.max(jnp.where(hit, key, 0), axis=1, keepdims=True)
-    req_s[...] = (jnp.where(col == 0, kmin, kmax) & 255).reshape(N, 1, N)
+    req_s[...] = (jnp.where(col == 0, kmin, kmax) & 255).reshape(8, 16, 1, N)
     slot_v[...] = own * 2 + jnp.sum(jnp.where(hit & (key != kmin), 1, 0), axis=0, keepdims=True)
-    pl.semaphore_wait(barrier, N - 1)
-    me = lax.axis_index("dom") * 8 + lax.axis_index("tool")
-    _, after, _ = peer(1)
-    _, before, _ = peer(N - 1)
-    down = pltpu.make_async_remote_copy(vec_h.at[pl.ds(56, 8)], lo, hs.at[0], hr.at[0], device_id=after, device_id_type=MESH)
-    up = pltpu.make_async_remote_copy(vec_h.at[pl.ds(0, 8)], hi, hs.at[1], hr.at[1], device_id=before, device_id_type=MESH)
-    local(req_s.at[me], req_r.at[me], rs1).start()
-
-    def send(j, c):
-        d, where, me = peer(j)
-        pltpu.make_async_remote_copy(req_s.at[d], req_r.at[me], ss1, rs1, device_id=where, device_id_type=MESH).start()
-        return c
-
-    lax.fori_loop(1, N, send, 0)
+    loads[2].wait()
+    prep_act(act, at, dw)
+    loads[3].wait()
+    vww = vw.at[pl.ds(192, 68 * 32)]
+
+    def relay(g, c):
+        to_w(vec[rows8(g), :], vw, 256 + g * 256)
+        return c
+
+    lax.fori_loop(0, 8, relay, 0)
+    pl.semaphore_wait(barrier, 24)
+    local(req_s.at[tl], req_m.at[tl], rs1).start()
+    for where in part:
+        remote(req_s.at[where[1]], req_m.at[tl], ss1, rs1, where).start()
+    down = remote(vec_h.at[pl.ds(56, 8)], lo, hs.at[0], hr.at[0], after)
+    up = remote(vec_h.at[pl.ds(0, 8)], hi, hs.at[1], hr.at[1], before)
     down.start()
     up.start()
     keep = local(slot_v, slot, ls.at[7])
     keep.start()
-    loads[3].wait()
-    loads[6].wait()
-    prep_act(act, at, dw)
-    vww = vw.at[pl.ds(192, 68 * 32)]
-
-    def relay(g, c):
-        to_w(vec[rows8(g), :], vw, 256 + g * 256)
-        return c
-
-    lax.fori_loop(0, 8, relay, 0)
 
     def pv(g, c):
         for u in range(4):
@@ -231,8 +223,23 @@
         return c
 
     lax.fori_loop(0, 16, pv, 0)
-    loads[2].wait()
-    local(req_r, req_r, rs1).wait()
+    local(req_m, req_m, rs1).wait()
+    local(req_m.at[:, dom], req_r.at[dom], rs3).start()
+    for where in span:
+        remote(req_m.at[:, where[0]], req_r.at[dom], ss3, rs3, where).start()
+    loads[4].wait()
+    for b0 in range(8):
+        for f in range(4):
+            rw[pl.ds(b0 * 32 + f, 8, stride=4), :] = rec[b0 * 8:b0 * 8 + 8, f * 128:(f + 1) * 128]
+
+    def pp(g, c):
+        for u in range(2):
+            prep_part(rw, ft, lhs, g * 2 + u, u)
+        return c
+
+    lax.fori_loop(0, 16, pp, 0)
+    loads[5].wait()
+    local(req_r, req_r, rs3).wait()
     ask = req_r[...].reshape(N, N)
     for r in range(2):
         hot = (iota((N, 256), 1) == ask[:, r:r + 1]).astype(F32)
@@ -242,11 +249,11 @@
     local(resp.at[me], got.at[me], rs2).start()
 
     def reply(j, c):
-        d, where, me = peer(j)
-        pltpu.make_async_remote_copy(resp.at[d], got.at[me], ss2, rs2, device_id=where, device_id_type=MESH).start()
-        return c
-
-    lax.fori_loop(1, N, reply, 0)
+        d = lax.rem(me + j, N)
+        remote(resp.at[d], got.at[me], ss2, rs2, (d // 8, lax.rem(d, 8))).start()
+        return c
+
+    lax.fori_loop(1, N, reply, 0, unroll=2)
     down.wait()
     up.wait()
 
@@ -262,18 +269,7 @@
     to_w(hi, vw, 256 + 2048)
     for i, c in enumerate((0, 1, 66, 67)):
         prep_vec(vww, nat.at[i], bv, c, None, vt, dw)
-    loads[5].wait()
-    for b0 in range(8):
-        for f in range(4):
-            rw[pl.ds(b0 * 32 + f, 8, stride=4), :] = rec[b0 * 8:b0 * 8 + 8, f * 128:(f + 1) * 128]
-
-    def pp(g, c):
-        for u in range(2):
-            prep_part(rw, ft, lhs, g * 2 + u, u)
-        return c
-
-    lax.fori_loop(0, 16, pp, 0)
-    loads[4].wait()
+    loads[6].wait()
 
     def ig(g, c):
         stiff(g).wait()
@@ -285,7 +281,8 @@
 
     lax.fori_loop(0, 8, ig, 0)
     keep.wait()
-    local(req_s.at[pl.ds(0, N - 1)], req_s.at[pl.ds(0, N - 1)], ss1).wait()
+    local(req_s.at[pl.ds(0, 7)], req_s.at[pl.ds(0, 7)], ss1).wait()
+    local(req_r.at[pl.ds(0, 15)], req_r.at[pl.ds(0, 15)], ss3).wait()
     local(got, got, rs2).wait()
 
     def cg(g, c):
@@ -300,37 +297,56 @@
         return c
 
     lax.fori_loop(0, NB // UC, cg, 0)
+    local(resp.at[pl.ds(0, N - 1)], resp.at[pl.ds(0, N - 1)], ss2).wait()
+
+
+def layout_kernel(iw, out_h, out, os):
+    def save(g):
+        return local(out.at[rows8(g), :], out_h.at[rows8(g), :], os.at[g])
 
     def og(g, c):
         for t in range(32):
             out[rows8(g), t * 128:(t + 1) * 128] = iw[pl.ds(g * 256 + t, 8, stride=32), :]
+        save(g).start()
         return c
 
     lax.fori_loop(0, 8, og, 0)
-    local(resp.at[pl.ds(0, N - 1)], resp.at[pl.ds(0, N - 1)], ss2).wait()
+    for g in range(8):
+        save(g).wait()
 
 
 def per_device(records, tool_data, owners, local_seg, active, stiffness, columns, vectors):
     vm, sm, dma = pltpu.VMEM, pltpu.SMEM, pltpu.SemaphoreType.DMA
     i32 = jnp.int32
-    return pl.pallas_call(
-        kernel,
-        out_shape=jax.ShapeDtypeStruct((NB, 4096), F32),
-        in_specs=[pl.BlockSpec(memory_space=pl.ANY)] * 8,
-        out_specs=pl.BlockSpec(memory_space=vm),
+    whole = pl.BlockSpec(memory_space=vm)
+    far = pl.BlockSpec(memory_space=pl.ANY)
+    iw = pl.pallas_call(
+        gather_kernel,
+        out_shape=jax.ShapeDtypeStruct((NB * 32, 128), F32),
+        in_specs=[far] * 8,
+        out_specs=whole,
         scratch_shapes=[
             vm((2, NB), i32), vm((2, NB), i32), vm((256, 512), F32), vm((NB, 4096), F32), sm((E5, NB), i32),
             vm((NB, 512), F32), vm((NB, 64), i32), vm((E5, NB, 4096), F32), vm((1, N), i32), sm((1, N), i32),
-            vm((N, 1, N), i32), vm((N, 1, N), i32), vm((N, 8, 128), F32), vm((N, 8, 128), F32),
+            vm((8, 16, 1, N), i32), vm((8, 16, 1, N), i32), vm((16, 8, 1, N), i32), vm((N, 8, 128), F32), vm((N, 8, 128), F32),
             vm((8, 4096), F32), vm((8, 4096), F32),
             vm((E5, 256, 128), F32), vm((80 * 32, 128), F32), vm((4, 64, 128), F32), vm((68, 128, 256), BF16),
             vm((NB, 64, 192), BF16), vm((64, 64), F32), vm((NB, 32, 128), F32), vm((256, 128), F32),
-            vm((3, 2, 128, 64), F32), vm((NB, 192, 64), BF16), vm((2048, 128), F32),
-            dma((8,)), dma((8,)), dma, dma, dma, dma, dma((2,)), dma((2,)),
+            vm((3, 2, 128, 64), F32), vm((NB, 192, 64), BF16),
+            dma((8,)), dma((8,)), dma, dma, dma, dma, dma, dma, dma((2,)), dma((2,)),
         ],
         compiler_params=pltpu.CompilerParams(collective_id=0, has_side_effects=True, vmem_limit_bytes=60 << 20),
-        name="mortar",
+        name="gather_rows",
     )(owners.T, local_seg.T, tool_data, vectors, columns.T, records, active, stiffness.transpose(1, 0, 2))
+    return pl.pallas_call(
+        layout_kernel,
+        out_shape=jax.ShapeDtypeStruct((NB, 4096), F32),
+        in_specs=[whole],
+        out_specs=far,
+        scratch_shapes=[vm((NB, 4096), F32), dma((8,))],
+        compiler_params=pltpu.CompilerParams(vmem_limit_bytes=16 << 20),
+        name="layout",
+    )(iw)
 
 
 def solution(mesh):

time: 48.4 us -> 38.8 us (0.80)
  Pallas kernels: 46 us -> 37.3 us
  local copies, waits for them, and re-layouts: 2.27 us -> 1.22 us
    pallas_call x1 -> x2, Pallas kernels: 46 us -> 37.3 us  [the longest x1 35.9 us: per_device(): pl.pallas_call(gather_kernel, out_shape=jax.ShapeDtypeStruct((NB * 32, 12...]
    unnamed x1 -> x2, local copies, waits for them, and re-layouts: 2.27 us -> 1.22 us
where the time goes in v2:
time: 38.8 us; the launch traced here: 38.5 us
  Pallas kernels  37.3 us (96%)
  local copies, waits for them, and re-layouts  1.22 us (3%)
    pallas_call x1, Pallas kernels, per_device(): pl.pallas_call(gather_kernel, out_shape=jax.ShapeDtypeStruct((NB * 32, 12...  35.9 us
    pallas_call x1, Pallas kernels, per_device(): pl.pallas_call(layout_kernel, out_shape=jax.ShapeDtypeStruct((NB, 4096),...  1.37 us
    unnamed x2, local copies, waits for them, and re-layouts  1.22 us

profile of v2, /device:TPU:1, one launch (start us, length us, event | category | flops | bytes accessed | tf_op | source)
XLA Modules:
  0.0 38.5 jit_solution(16607014098559196322)
XLA Ops:
  0.0 35.9 %gather_rows.1.iw = f32[2048,128]{1,0:T(8,128)} custom-call(s32[2,64]{1,0:T(2,128)} %bitcast.6, s32[2,64]{1,0:T(2,128)} %bitcast.7, f32[256,512]{1,0:T(8,128)} %tool_h.1, f32[64,4096]{1,0:T(8,128)} %vec_h.1, s32[5,64]{1,0:T(8,128)} %bitcast.5, f32[64,512]{1,0:T(8,128)} %rec_h.1, s32[64,64]{1,0:T(8,128)} %act_h.1, f32[5,64,4096]{2,1,0:T(8,128)} %bitcast.4), custom_call_target="tpu_custom_call" | custom-call | tf_op jit(solution)/shard_map/gather_rows/pallas_call | solution.py:323
  35.9 0.0 copy-start
  36.0 1.2 %copy-done = f32[2048,128]{1,0:T(8,128)S(1)} copy-done((f32[2048,128]{1,0:T(8,128)S(1)}, f32[2048,128]{1,0:T(8,128)}, u32[]{:S(2)}) %copy-start) | copy-done | bytes 1048600
  37.2 1.4 %layout.1 = f32[64,4096]{1,0:T(8,128)} custom-call(f32[2048,128]{1,0:T(8,128)S(1)} %copy-done), custom_call_target="tpu_custom_call" | custom-call | tf_op jit(solution)/shard_map/layout/pallas_call | solution.py:341
Async XLA Ops:
  35.9 1.2 %copy-start = (f32[2048,128]{1,0:T(8,128)S(1)}, f32[2048,128]{1,0:T(8,128)}, u32[]{:S(2)}) copy-start(f32[2048,128]{1,0:T(8,128)} %gather_rows.1.iw) | copy-start | bytes 3145732

commit v3 on v2

--- a/solution.py
+++ b/solution.py
@@ -33,10 +33,6 @@
     m = y.astype(BF16).astype(F32)
     return h, m, y - m
 
-def to_w(src, dst, row0):
-    for t in range(32):
-        dst[pl.ds(row0 + t, 8, stride=32), :] = src[:, t * 128:(t + 1) * 128]
-
 def pair8(g0, g1):
     lane = iota((4, 128), 1)
     ev = jnp.where(lane < 64, g0, pltpu.roll(g1, 64, 1))
@@ -53,8 +49,7 @@
 def square_sum(x):
     return jnp.sum(jnp.where(mask_rows((0, 1, 4)), x * x, 0.0), 0, keepdims=True) * A2
 
-def prep_vec(vw, nat, bv, c, own_b, vt, dw):
-    w = vw[pl.ds(pl.multiple_of(c * 32, 32), 32), :]
+def prep_vec(w, nat, bv, c, own_b, vt, dw):
     lane = iota((32, 128), 1)
     wr = pltpu.roll(w, 64, 1)
     nat[pl.ds(0, 32, stride=2), :] = jnp.where(lane < 64, w, wr)
@@ -78,16 +73,15 @@
     row, col = iota((128, 128), 0), iota((128, 128), 1)
     same = (row // 64) == (col // 64)
     def one(g, carry):
-        for k in range(4):
-            b = g * 4 + k
+        for k in range(16):
+            b = g * 16 + k
             hot = jnp.where(same & (lax.rem(row, 64) == b), 1.0, 0.0).astype(BF16)
             dw[b] = jnp.dot(a, hot, preferred_element_type=F32)
         return carry
-    lax.fori_loop(0, 16, one, 0)
+    lax.fori_loop(0, 4, one, 0)
 
 def prep_part(rw, ft, lhs, g, k):
-    r4 = rw[pl.ds(pl.multiple_of(g * 8, 8), 8), :]
-    p = pair8(r4[0:4], r4[4:8])
+    p = pair8(rw[g // 4, lax.rem(g, 4) * 2], rw[g // 4, lax.rem(g, 4) * 2 + 1])
     sub = iota((8, 128), 0)
     pos = mask_rows((0, 1, 4))
     ph, pm, pl_ = split3(-square_sum(p))
@@ -106,12 +100,13 @@
                 parts.append(ft[n, k, pl.ds(q * 64 + par, 32, stride=2), :])
         lhs[g * 2 + q] = jnp.concatenate(parts, 0).astype(BF16)
 
-def inner_block(cols, sw, bv, iw, b, bb):
-    w = jnp.concatenate([sw[e, bb * 32:(bb + 1) * 32, :] for e in range(E5)], 1)
+def inner_block(cols, sw, bv, b, bb):
+    w = jnp.concatenate([sw[e, b // 8, bb] for e in range(E5)], 1)
     h, l = split(w)
     r = jnp.concatenate([bv[cols[e, b]] for e in range(E5)], 0)
     o = jnp.dot(jnp.concatenate([h, l], 0), r, preferred_element_type=F32)
-    iw[pl.ds(pl.multiple_of(b * 32, 32), 32), :] = (o[:32, :128] + o[:32, 128:]) + (o[32:, :128] + o[32:, 128:])
+    return (o[:32, :128] + o[:32, 128:]) + (o[32:, :128] + o[32:, 128:])
+
 
 def cand_rows(got, s):
     x = got[s // 2]
@@ -160,20 +155,20 @@
     return pltpu.make_async_remote_copy(src, dst, send, recv, device_id=where, device_id_type=MESH)
 
 
-def gather_kernel(own_h, seg_h, tool_h, vec_h, cols_h, rec_h, act_h, s_h, iw,
-                  own_v, seg_v, tool, vec, cols, rec, act, s_v, slot_v, slot,
-                  req_s, req_m, req_r, resp, got, lo, hi, sw, vw, nat, bv, vt, at, dw, rw, ft, lhs,
-                  ls, gs, ss1, rs1, ss2, rs2, ss3, rs3, hs, hr):
+def gather_kernel(own_h, seg_h, tool_h, vec_h, cols_h, rec_h, act_h, s_h, iw_h,
+                  own_v, seg_v, tool, vw, cols, rw, act, sw, slot_v, slot,
+                  req_s, req_m, req_r, resp, got, lo, hi, iw, nat, bv, vt, at, dw, ft, lhs,
+                  ls, ws, vs, fs, gs, ss1, rs1, ss2, rs2, ss3, rs3, hs, hr):
     loads = [local(a, b, ls.at[i]) for i, (a, b) in enumerate(
-        ((own_h, own_v), (seg_h, seg_v), (act_h, act), (vec_h, vec), (rec_h, rec), (tool_h, tool), (cols_h, cols)))]
-    for c in loads:
+        ((own_h, own_v), (seg_h, seg_v), (act_h, act), (tool_h, tool), (cols_h, cols)))]
+    for c in loads[:3]:
         c.start()
-
-    def stiff(g):
-        return local(s_h.at[:, rows8(g), :], s_v.at[:, rows8(g), :], gs.at[g])
-
-    for g in range(8):
-        stiff(g).start()
+    for k in range(8):
+        local(vec_h.at[:, :, k], vw.at[:, k], vs).start()
+    for k in range(8):
+        local(rec_h.at[:, :, k], rw.at[:, k], fs).start()
+    for c in loads[3:]:
+        c.start()
     dom, tl = lax.axis_index("dom"), lax.axis_index("tool")
     me = dom * 8 + tl
     px, py = dom // 4, lax.rem(dom, 4)
@@ -185,6 +180,8 @@
     barrier = pltpu.get_barrier_semaphore()
     for where in span + part + [after, before]:
         pl.semaphore_signal(barrier, inc=1, device_id=where, device_id_type=MESH)
+    for k in range(8):
+        local(s_h.at[:, :, :, k], sw.at[:, :, k], gs).start()
     loads[0].wait()
     loads[1].wait()
     own = jnp.concatenate([own_v[0:1, :], own_v[1:2, :]], axis=1)
@@ -198,28 +195,23 @@
     slot_v[...] = own * 2 + jnp.sum(jnp.where(hit & (key != kmin), 1, 0), axis=0, keepdims=True)
     loads[2].wait()
     prep_act(act, at, dw)
-    loads[3].wait()
-    vww = vw.at[pl.ds(192, 68 * 32)]
-
-    def relay(g, c):
-        to_w(vec[rows8(g), :], vw, 256 + g * 256)
-        return c
-
-    lax.fori_loop(0, 8, relay, 0)
     pl.semaphore_wait(barrier, 24)
     local(req_s.at[tl], req_m.at[tl], rs1).start()
     for where in part:
         remote(req_s.at[where[1]], req_m.at[tl], ss1, rs1, where).start()
-    down = remote(vec_h.at[pl.ds(56, 8)], lo, hs.at[0], hr.at[0], after)
-    up = remote(vec_h.at[pl.ds(0, 8)], hi, hs.at[1], hr.at[1], before)
-    down.start()
-    up.start()
+    halo = [remote(vec_h.at[7, :, 6 + k], lo.at[k], hs.at[k], hr.at[k], after) for k in range(HB)]
+    halo += [remote(vec_h.at[0, :, k], hi.at[k], hs.at[HB + k], hr.at[HB + k], before) for k in range(HB)]
+    for c in halo:
+        c.start()
     keep = local(slot_v, slot, ls.at[7])
     keep.start()
 
+    local(vw, vw, vs).wait()
+
     def pv(g, c):
         for u in range(4):
-            prep_vec(vww, nat.at[u], bv, g * 4 + u + 2, g * 4 + u, vt, dw)
+            b = g * 4 + u
+            prep_vec(vw[g // 2, lax.rem(g, 2) * 4 + u], nat.at[u], bv, b + HB, b, vt, dw)
         return c
 
     lax.fori_loop(0, 16, pv, 0)
@@ -227,18 +219,15 @@
     local(req_m.at[:, dom], req_r.at[dom], rs3).start()
     for where in span:
         remote(req_m.at[:, where[0]], req_r.at[dom], ss3, rs3, where).start()
-    loads[4].wait()
-    for b0 in range(8):
-        for f in range(4):
-            rw[pl.ds(b0 * 32 + f, 8, stride=4), :] = rec[b0 * 8:b0 * 8 + 8, f * 128:(f + 1) * 128]
+    local(rw, rw, fs).wait()
 
     def pp(g, c):
-        for u in range(2):
-            prep_part(rw, ft, lhs, g * 2 + u, u)
-        return c
-
-    lax.fori_loop(0, 16, pp, 0)
-    loads[5].wait()
+        for u in range(4):
+            prep_part(rw, ft, lhs, g * 4 + u, u)
+        return c
+
+    lax.fori_loop(0, 8, pp, 0)
+    loads[3].wait()
     local(req_r, req_r, rs3).wait()
     ask = req_r[...].reshape(N, N)
     for r in range(2):
@@ -254,8 +243,8 @@
         return c
 
     lax.fori_loop(1, N, reply, 0, unroll=2)
-    down.wait()
-    up.wait()
+    for c in halo:
+        c.wait()
 
     @pl.when(me == 0)
     def _():
@@ -265,18 +254,16 @@
     def _():
         hi[...] = jnp.zeros_like(hi)
 
-    to_w(lo, vw, 0)
-    to_w(hi, vw, 256 + 2048)
-    for i, c in enumerate((0, 1, 66, 67)):
-        prep_vec(vww, nat.at[i], bv, c, None, vt, dw)
-    loads[6].wait()
+    for k in range(HB):
+        prep_vec(lo[k], nat.at[k], bv, k, None, vt, dw)
+        prep_vec(hi[k], nat.at[HB + k], bv, HB + NB + k, None, vt, dw)
+    loads[4].wait()
+    local(sw, sw, gs).wait()
 
     def ig(g, c):
-        stiff(g).wait()
-        for e in range(E5):
-            to_w(s_v[e, rows8(g), :], sw.at[e], 0)
-        for bb in range(8):
-            inner_block(cols, sw, bv, iw, g * 8 + bb, bb)
+        z = [inner_block(cols, sw, bv, g * 8 + u, u) for u in range(8)]
+        for u in range(8):
+            iw[g, u] = z[u]
         return c
 
     lax.fori_loop(0, 8, ig, 0)
@@ -285,68 +272,80 @@
     local(req_r.at[pl.ds(0, 15)], req_r.at[pl.ds(0, 15)], ss3).wait()
     local(got, got, rs2).wait()
 
+    def leave(g):
+        block = pl.ds(g * (UC // 8), UC // 8)
+        return local(iw.at[block], iw_h.at[block], ws.at[g])
+
     def cg(g, c):
         bs = [g * UC + u for u in range(UC)]
         t = [tile_of(slot, got, lhs, b) for b in bs]
         y = [first(vt, b, *x) for b, x in zip(bs, t)]
         z = [second(dw, b, *x, *w) for b, x, w in zip(bs, t, y)]
-        at32 = [pl.ds(pl.multiple_of(b * 32, 32), 32) for b in bs]
-        total = [iw[a, :] + w for a, w in zip(at32, z)]
-        for a, w in zip(at32, total):
-            iw[a, :] = w
+        spot = [(g * (UC // 8) + u // 8, u % 8) for u in range(UC)]
+        total = [iw[p] + w for p, w in zip(spot, z)]
+        for p, w in zip(spot, total):
+            iw[p] = w
+        leave(g).start()
         return c
 
     lax.fori_loop(0, NB // UC, cg, 0)
+    for g in range(NB // UC):
+        leave(g).wait()
     local(resp.at[pl.ds(0, N - 1)], resp.at[pl.ds(0, N - 1)], ss2).wait()
 
 
-def layout_kernel(iw, out_h, out, os):
-    def save(g):
-        return local(out.at[rows8(g), :], out_h.at[rows8(g), :], os.at[g])
-
-    def og(g, c):
-        for t in range(32):
-            out[rows8(g), t * 128:(t + 1) * 128] = iw[pl.ds(g * 256 + t, 8, stride=32), :]
-        save(g).start()
-        return c
-
-    lax.fori_loop(0, 8, og, 0)
-    for g in range(8):
-        save(g).wait()
+def layout_kernel(iw_h, out_h, iw, ws, os):
+    def load(k):
+        return local(iw_h.at[:, k], iw.at[:, k], ws.at[k])
+
+    def save(k):
+        return local(iw.at[:, k], out_h.at[:, :, k], os.at[k])
+
+    for k in range(8):
+        load(k).start()
+    for k in range(8):
+        load(k).wait()
+        save(k).start()
+    for k in range(8):
+        save(k).wait()
+
+
+def sublanes_last(x):
+    return x.reshape(8, 8, -1, 128).transpose(0, 2, 1, 3)
 
 
 def per_device(records, tool_data, owners, local_seg, active, stiffness, columns, vectors):
     vm, sm, dma = pltpu.VMEM, pltpu.SMEM, pltpu.SemaphoreType.DMA
     i32 = jnp.int32
-    whole = pl.BlockSpec(memory_space=vm)
     far = pl.BlockSpec(memory_space=pl.ANY)
     iw = pl.pallas_call(
         gather_kernel,
-        out_shape=jax.ShapeDtypeStruct((NB * 32, 128), F32),
+        out_shape=jax.ShapeDtypeStruct((8, 8, 32, 128), F32),
         in_specs=[far] * 8,
-        out_specs=whole,
+        out_specs=far,
         scratch_shapes=[
-            vm((2, NB), i32), vm((2, NB), i32), vm((256, 512), F32), vm((NB, 4096), F32), sm((E5, NB), i32),
-            vm((NB, 512), F32), vm((NB, 64), i32), vm((E5, NB, 4096), F32), vm((1, N), i32), sm((1, N), i32),
+            vm((2, NB), i32), vm((2, NB), i32), vm((256, 512), F32), vm((8, 8, 32, 128), F32), sm((E5, NB), i32),
+            vm((8, 8, 4, 128), F32), vm((NB, 64), i32), vm((E5, 8, 8, 32, 128), F32), vm((1, N), i32), sm((1, N), i32),
             vm((8, 16, 1, N), i32), vm((8, 16, 1, N), i32), vm((16, 8, 1, N), i32), vm((N, 8, 128), F32), vm((N, 8, 128), F32),
-            vm((8, 4096), F32), vm((8, 4096), F32),
-            vm((E5, 256, 128), F32), vm((80 * 32, 128), F32), vm((4, 64, 128), F32), vm((68, 128, 256), BF16),
-            vm((NB, 64, 192), BF16), vm((64, 64), F32), vm((NB, 32, 128), F32), vm((256, 128), F32),
-            vm((3, 2, 128, 64), F32), vm((NB, 192, 64), BF16),
-            dma((8,)), dma((8,)), dma, dma, dma, dma, dma, dma, dma((2,)), dma((2,)),
+            vm((HB, 32, 128), F32), vm((HB, 32, 128), F32), vm((8, 8, 32, 128), F32),
+            vm((4, 64, 128), F32), vm((68, 128, 256), BF16), vm((NB, 64, 192), BF16), vm((64, 64), F32),
+            vm((NB, 32, 128), F32), vm((3, 4, 128, 64), F32), vm((NB, 192, 64), BF16),
+            dma((8,)), dma((NB // UC,)), dma, dma, dma, dma, dma, dma, dma, dma, dma, dma((2 * HB,)), dma((2 * HB,)),
         ],
         compiler_params=pltpu.CompilerParams(collective_id=0, has_side_effects=True, vmem_limit_bytes=60 << 20),
         name="gather_rows",
-    )(owners.T, local_seg.T, tool_data, vectors, columns.T, records, active, stiffness.transpose(1, 0, 2))
-    return pl.pallas_call(
+    )(owners.T, local_seg.T, tool_data, sublanes_last(vectors), columns.T, sublanes_last(records), active,
+      stiffness.transpose(1, 0, 2).reshape(E5, 8, 8, 32, 128).transpose(0, 1, 3, 2, 4))
+    out = pl.pallas_call(
         layout_kernel,
-        out_shape=jax.ShapeDtypeStruct((NB, 4096), F32),
-        in_specs=[whole],
+        out_shape=jax.ShapeDtypeStruct((8, 32, 8, 128), F32),
+        in_specs=[far],
         out_specs=far,
-        scratch_shapes=[vm((NB, 4096), F32), dma((8,))],
-        compiler_params=pltpu.CompilerParams(vmem_limit_bytes=16 << 20),
+        scratch_shapes=[vm((8, 8, 32, 128), F32), dma((8,)), dma((8,))],
+        compiler_params=pltpu.CompilerParams(vmem_limit_bytes=60 << 20),
         name="layout",
     )(iw)
+    return out.transpose(0, 2, 1, 3).reshape(NB, 4096)
 
 
 def solution(mesh):

time: 38.8 us -> 35.8 us (0.923)
  Pallas kernels: 37.3 us -> 35.7 us
  local copies, waits for them, and re-layouts: 1.22 us -> 0 us
    pallas_call x2, Pallas kernels: 37.3 us -> 35.7 us  [the longest x1 33.6 us: per_device(): pl.pallas_call(gather_kernel, out_shape=jax.ShapeDtypeStruct((8, 8, 32, 1...]
    unnamed x2 -> x0, local copies, waits for them, and re-layouts: 1.22 us -> none
where the time goes in v3:
time: 35.8 us; the launch traced here: 35.7 us
  Pallas kernels  35.7 us (100%)
    pallas_call x1, Pallas kernels, per_device(): pl.pallas_call(gather_kernel, out_shape=jax.ShapeDtypeStruct((8, 8, 32, 1...  33.6 us
    pallas_call x1, Pallas kernels, per_device(): pl.pallas_call(layout_kernel, out_shape=jax.ShapeDtypeStruct((8, 32, 8, 1...  2.09 us

profile of v3, /device:TPU:1, one launch (start us, length us, event | category | flops | bytes accessed | tf_op | source)
XLA Modules:
  0.0 35.7 jit_solution(11091227097156532721)
XLA Ops:
  0.0 33.6 %gather_rows.1.iw_h = f32[8,8,32,128]{3,2,1,0:T(8,128)} custom-call(s32[2,64]{1,0:T(2,128)} %bitcast.21, s32[2,64]{1,0:T(2,128)} %bitcast.22, f32[256,512]{1,0:T(8,128)} %tool_h.1, f32[8,32,8,128]{3,2,1,0:T(8,128)} %bitcast.18, s32[5,64]{1,0:T(8,128)} %bitcast.20, f32[8,4,8,128]{3,2,1,0:T(8,128)} %bitcast.19, s32[64,64]{1,0:T(8,128)} %act_h.1, ...), custom_call_target="tpu_custom_call" | custom-call | tf_op jit(solution)/shard_map/gather_rows/pallas_call | solution.py:321
  33.6 2.1 %layout.1 = f32[8,32,8,128]{3,2,1,0:T(8,128)} custom-call(f32[8,8,32,128]{3,2,1,0:T(8,128)} %gather_rows.1.iw_h), custom_call_target="tpu_custom_call" | custom-call | tf_op jit(solution)/shard_map/layout/pallas_call | solution.py:339

commit v4 on v3

--- a/solution.py
+++ b/solution.py
@@ -112,8 +112,8 @@
     x = got[s // 2]
     return jnp.where(lax.rem(s, 2) == 1, x[4:8], x[0:4])
 
-def tile_of(slot, got, lhs, b):
-    x = pair8(cand_rows(got, slot[0, b]), cand_rows(got, slot[0, NB + b]))
+def tile_of(xt, lhs, b):
+    x = xt[b]
     sub = iota((8, 128), 0)
     h, m, l = split3(x)
     qh, qm, ql = split3(square_sum(x))
@@ -140,7 +140,9 @@
 
 MESH = pl.DeviceIdType.MESH
 N = 128
-UC = 16
+UC = 32
+PV = 12
+RINGS = (((1, 0), (3, 0), (0, 1), (0, 3), (0, 0)), ((2, 0), (0, 2), (1, 1), (1, 3), (3, 1), (3, 3)), ((2, 1), (2, 3), (1, 2), (3, 2)), ((2, 2),))
 
 
 def rows8(g):
@@ -155,19 +157,13 @@
     return pltpu.make_async_remote_copy(src, dst, send, recv, device_id=where, device_id_type=MESH)
 
 
-def gather_kernel(own_h, seg_h, tool_h, vec_h, cols_h, rec_h, act_h, s_h, iw_h,
+def gather_kernel(own_h, seg_h, tool_h, vec_h, cols_h, rec_h, act_h, s_h, xt, lhs, vt, dw, iw,
                   own_v, seg_v, tool, vw, cols, rw, act, sw, slot_v, slot,
-                  req_s, req_m, req_r, resp, got, lo, hi, iw, nat, bv, vt, at, dw, ft, lhs,
-                  ls, ws, vs, fs, gs, ss1, rs1, ss2, rs2, ss3, rs3, hs, hr):
+                  req_s, req_m, req_r, resp, got, lo, hi, nat, bv, at, ft, tool3,
+                  ls, vs, fs, gs, ss1, rs1, ss2, rs2, ss3, rs3, hs, hr):
     loads = [local(a, b, ls.at[i]) for i, (a, b) in enumerate(
         ((own_h, own_v), (seg_h, seg_v), (act_h, act), (tool_h, tool), (cols_h, cols)))]
-    for c in loads[:3]:
-        c.start()
-    for k in range(8):
-        local(vec_h.at[:, :, k], vw.at[:, k], vs).start()
-    for k in range(8):
-        local(rec_h.at[:, :, k], rw.at[:, k], fs).start()
-    for c in loads[3:]:
+    for c in loads[:2]:
         c.start()
     dom, tl = lax.axis_index("dom"), lax.axis_index("tool")
     me = dom * 8 + tl
@@ -180,6 +176,12 @@
     barrier = pltpu.get_barrier_semaphore()
     for where in span + part + [after, before]:
         pl.semaphore_signal(barrier, inc=1, device_id=where, device_id_type=MESH)
+    for c in loads[2:]:
+        c.start()
+    for k in range(8):
+        local(vec_h.at[:, :, k], vw.at[:, k], vs).start()
+    for k in range(8):
+        local(rec_h.at[:, :, k], rw.at[:, k], fs).start()
     for k in range(8):
         local(s_h.at[:, :, :, k], sw.at[:, :, k], gs).start()
     loads[0].wait()
@@ -192,7 +194,10 @@
     kmin = jnp.min(jnp.where(hit, key, 1 << 20), axis=1, keepdims=True)
     kmax = jnp.max(jnp.where(hit, key, 0), axis=1, keepdims=True)
     req_s[...] = (jnp.where(col == 0, kmin, kmax) & 255).reshape(8, 16, 1, N)
-    slot_v[...] = own * 2 + jnp.sum(jnp.where(hit & (key != kmin), 1, 0), axis=0, keepdims=True)
+    loads[3].wait()
+    for k in range(4):
+        for n, x in enumerate(split3(tool[k * 64:(k + 1) * 64, :])):
+            tool3[k * 64:(k + 1) * 64, n * 512:(n + 1) * 512] = x.astype(BF16)
     loads[2].wait()
     prep_act(act, at, dw)
     pl.semaphore_wait(barrier, 24)
@@ -203,8 +208,7 @@
     halo += [remote(vec_h.at[0, :, k], hi.at[k], hs.at[HB + k], hr.at[HB + k], before) for k in range(HB)]
     for c in halo:
         c.start()
-    keep = local(slot_v, slot, ls.at[7])
-    keep.start()
+    slot_v[...] = own * 2 + jnp.sum(jnp.where(hit & (key != kmin), 1, 0), axis=0, keepdims=True)
 
     local(vw, vw, vs).wait()
 
@@ -214,11 +218,46 @@
             prep_vec(vw[g // 2, lax.rem(g, 2) * 4 + u], nat.at[u], bv, b + HB, b, vt, dw)
         return c
 
-    lax.fori_loop(0, 16, pv, 0)
+    lax.fori_loop(0, PV, pv, 0)
     local(req_m, req_m, rs1).wait()
-    local(req_m.at[:, dom], req_r.at[dom], rs3).start()
+    local(req_m.at[:, dom], req_r.at[dom], rs3.at[dom]).start()
     for where in span:
-        remote(req_m.at[:, where[0]], req_r.at[dom], ss3, rs3, where).start()
+        remote(req_m.at[:, where[0]], req_r.at[dom], ss3, rs3.at[dom], where).start()
+    keep = local(slot_v, slot, ls.at[7])
+    keep.start()
+    lax.fori_loop(PV, 16, pv, 0)
+    for ring in RINGS:
+        rows = [lax.rem(px + a, 4) * 4 + lax.rem(py + b, 4) for a, b in ring]
+        for d in rows:
+            local(req_r.at[d], req_r.at[d], rs3.at[d]).wait()
+        n = len(rows) * 8
+        ask = jnp.concatenate([req_r[d].reshape(8, N) for d in rows], 0)
+        hot = jnp.concatenate([(iota((n, 256), 1) == ask[:, r:r + 1]).astype(F32) for r in range(2)], 0).astype(BF16)
+        g = jnp.dot(hot, tool3[...], preferred_element_type=F32)
+        g = (g[:, :512] + g[:, 512:1024]) + g[:, 1024:]
+        for i, d in enumerate(rows):
+            for r in range(2):
+                for f in range(4):
+                    resp[rows8(d), r * 4 + f, :] = g[r * n + i * 8:r * n + i * 8 + 8, f * 128:(f + 1) * 128]
+        far = [d for d, at in zip(rows, ring) if at != (0, 0)]
+        near = len(far) < len(rows)
+        if near:
+            local(resp.at[me], got.at[me], rs2).start()
+
+        def reply(j, c, far=far, near=near):
+            t = lax.rem(tl + j, 8)
+            for d in far:
+                remote(resp.at[d * 8 + t], got.at[me], ss2, rs2, (d, t)).start()
+            return c
+
+        def beside(j, c):
+            t = lax.rem(tl + j, 8)
+            remote(resp.at[dom * 8 + t], got.at[me], ss2, rs2, (dom, t)).start()
+            return c
+
+        lax.fori_loop(0, 8, reply, 0)
+        if near:
+            lax.fori_loop(1, 8, beside, 0)
     local(rw, rw, fs).wait()
 
     def pp(g, c):
@@ -227,22 +266,6 @@
         return c
 
     lax.fori_loop(0, 8, pp, 0)
-    loads[3].wait()
-    local(req_r, req_r, rs3).wait()
-    ask = req_r[...].reshape(N, N)
-    for r in range(2):
-        hot = (iota((N, 256), 1) == ask[:, r:r + 1]).astype(F32)
-        g = jnp.dot(hot, tool[...], precision=lax.Precision.HIGHEST, preferred_element_type=F32)
-        for f in range(4):
-            resp[:, r * 4 + f, :] = g[:, f * 128:(f + 1) * 128]
-    local(resp.at[me], got.at[me], rs2).start()
-
-    def reply(j, c):
-        d = lax.rem(me + j, N)
-        remote(resp.at[d], got.at[me], ss2, rs2, (d // 8, lax.rem(d, 8))).start()
-        return c
-
-    lax.fori_loop(1, N, reply, 0, unroll=2)
     for c in halo:
         c.wait()
 
@@ -272,42 +295,36 @@
     local(req_r.at[pl.ds(0, 15)], req_r.at[pl.ds(0, 15)], ss3).wait()
     local(got, got, rs2).wait()
 
-    def leave(g):
-        block = pl.ds(g * (UC // 8), UC // 8)
-        return local(iw.at[block], iw_h.at[block], ws.at[g])
+    def pick(g, c):
+        for u in range(8):
+            b = g * 8 + u
+            xt[b] = pair8(cand_rows(got, slot[0, b]), cand_rows(got, slot[0, NB + b]))
+        return c
+
+    lax.fori_loop(0, 8, pick, 0)
+    local(resp.at[pl.ds(0, N - 1)], resp.at[pl.ds(0, N - 1)], ss2).wait()
+
+
+def contact_kernel(xt, lhs, vt, dw, iw, out_h, total, os):
+    def save(g, k):
+        return local(total.at[pl.ds(g * (UC // 8), UC // 8), k], out_h.at[pl.ds(g * (UC // 8), UC // 8), :, k], os.at[g, k])
 
     def cg(g, c):
         bs = [g * UC + u for u in range(UC)]
-        t = [tile_of(slot, got, lhs, b) for b in bs]
+        t = [tile_of(xt, lhs, b) for b in bs]
         y = [first(vt, b, *x) for b, x in zip(bs, t)]
         z = [second(dw, b, *x, *w) for b, x, w in zip(bs, t, y)]
-        spot = [(g * (UC // 8) + u // 8, u % 8) for u in range(UC)]
-        total = [iw[p] + w for p, w in zip(spot, z)]
-        for p, w in zip(spot, total):
-            iw[p] = w
-        leave(g).start()
+        for u, w in enumerate(z):
+            spot = (g * (UC // 8) + u // 8, u % 8)
+            total[spot] = iw[spot] + w
+        for k in range(8):
+            save(g, k).start()
         return c
 
     lax.fori_loop(0, NB // UC, cg, 0)
     for g in range(NB // UC):
-        leave(g).wait()
-    local(resp.at[pl.ds(0, N - 1)], resp.at[pl.ds(0, N - 1)], ss2).wait()
-
-
-def layout_kernel(iw_h, out_h, iw, ws, os):
-    def load(k):
-        return local(iw_h.at[:, k], iw.at[:, k], ws.at[k])
-
-    def save(k):
-        return local(iw.at[:, k], out_h.at[:, :, k], os.at[k])
-
-    for k in range(8):
-        load(k).start()
-    for k in range(8):
-        load(k).wait()
-        save(k).start()
-    for k in range(8):
-        save(k).wait()
+        for k in range(8):
+            save(g, k).wait()
 
 
 def sublanes_last(x):
@@ -318,33 +335,35 @@
     vm, sm, dma = pltpu.VMEM, pltpu.SMEM, pltpu.SemaphoreType.DMA
     i32 = jnp.int32
     far = pl.BlockSpec(memory_space=pl.ANY)
-    iw = pl.pallas_call(
+    whole = pl.BlockSpec(memory_space=vm)
+    parts = pl.pallas_call(
         gather_kernel,
-        out_shape=jax.ShapeDtypeStruct((8, 8, 32, 128), F32),
+        out_shape=(jax.ShapeDtypeStruct((NB, 8, 128), F32), jax.ShapeDtypeStruct((NB, 192, 64), BF16),
+                   jax.ShapeDtypeStruct((NB, 64, 192), BF16), jax.ShapeDtypeStruct((NB, 32, 128), F32),
+                   jax.ShapeDtypeStruct((8, 8, 32, 128), F32)),
         in_specs=[far] * 8,
-        out_specs=far,
+        out_specs=(whole,) * 5,
         scratch_shapes=[
             vm((2, NB), i32), vm((2, NB), i32), vm((256, 512), F32), vm((8, 8, 32, 128), F32), sm((E5, NB), i32),
             vm((8, 8, 4, 128), F32), vm((NB, 64), i32), vm((E5, 8, 8, 32, 128), F32), vm((1, N), i32), sm((1, N), i32),
             vm((8, 16, 1, N), i32), vm((8, 16, 1, N), i32), vm((16, 8, 1, N), i32), vm((N, 8, 128), F32), vm((N, 8, 128), F32),
-            vm((HB, 32, 128), F32), vm((HB, 32, 128), F32), vm((8, 8, 32, 128), F32),
-            vm((4, 64, 128), F32), vm((68, 128, 256), BF16), vm((NB, 64, 192), BF16), vm((64, 64), F32),
-            vm((NB, 32, 128), F32), vm((3, 4, 128, 64), F32), vm((NB, 192, 64), BF16),
-            dma((8,)), dma((NB // UC,)), dma, dma, dma, dma, dma, dma, dma, dma, dma, dma((2 * HB,)), dma((2 * HB,)),
+            vm((HB, 32, 128), F32), vm((HB, 32, 128), F32),
+            vm((4, 64, 128), F32), vm((68, 128, 256), BF16), vm((64, 64), F32), vm((3, 4, 128, 64), F32), vm((256, 1536), BF16),
+            dma((8,)), dma, dma, dma, dma, dma, dma, dma, dma, dma((16,)), dma((2 * HB,)), dma((2 * HB,)),
         ],
-        compiler_params=pltpu.CompilerParams(collective_id=0, has_side_effects=True, vmem_limit_bytes=60 << 20),
+        compiler_params=pltpu.CompilerParams(collective_id=0, has_side_effects=True, vmem_limit_bytes=28 << 20),
         name="gather_rows",
-    )(owners.T, local_seg.T, tool_data, sublanes_last(vectors), columns.T, sublanes_last(records), active,
-      stiffness.transpose(1, 0, 2).reshape(E5, 8, 8, 32, 128).transpose(0, 1, 3, 2, 4))
+    )(*[pltpu.with_memory_space_constraint(x, pltpu.HBM) for x in (owners.T, local_seg.T, tool_data, sublanes_last(vectors), columns.T, sublanes_last(records), active,
+      stiffness.transpose(1, 0, 2).reshape(E5, 8, 8, 32, 128).transpose(0, 1, 3, 2, 4))])
     out = pl.pallas_call(
-        layout_kernel,
+        contact_kernel,
         out_shape=jax.ShapeDtypeStruct((8, 32, 8, 128), F32),
-        in_specs=[far],
+        in_specs=[whole] * 5,
         out_specs=far,
-        scratch_shapes=[vm((8, 8, 32, 128), F32), dma((8,)), dma((8,))],
-        compiler_params=pltpu.CompilerParams(vmem_limit_bytes=60 << 20),
-        name="layout",
-    )(iw)
+        scratch_shapes=[vm((8, 8, 32, 128), F32), dma((NB // UC, 8))],
+        compiler_params=pltpu.CompilerParams(vmem_limit_bytes=24 << 20),
+        name="contact",
+    )(*parts)
     return out.transpose(0, 2, 1, 3).reshape(NB, 4096)
 
 

time: 35.8 us -> 33.1 us (0.925)
  Pallas kernels: 35.7 us -> 33 us
    pallas_call x2, Pallas kernels: 35.7 us -> 33 us  [the longest x1 27.7 us: per_device(): pl.pallas_call(gather_kernel, out_shape=(jax.ShapeDtypeStruct((NB, 8, 128...]
where the time goes in v4:
time: 33.1 us; the launch traced here: 33 us
  Pallas kernels  33 us (100%)
    pallas_call x1, Pallas kernels, per_device(): pl.pallas_call(gather_kernel, out_shape=(jax.ShapeDtypeStruct((NB, 8, 128...  27.7 us
    pallas_call x1, Pallas kernels, per_device(): pl.pallas_call(contact_kernel, out_shape=jax.ShapeDtypeStruct((8, 32, 8,...  5.37 us

profile of v4, /device:TPU:1, one launch (start us, length us, event | category | flops | bytes accessed | tf_op | source)
XLA Modules:
  0.0 33.0 jit_solution(10662020170159904243)
XLA Ops:
  0.0 27.7 %gather_rows.1 = (f32[64,8,128]{2,1,0:T(8,128)S(1)}, bf16[64,192,64]{2,1,0:T(8,128)(2,1)S(1)}, bf16[64,64,192]{2,1,0:T(8,128)(2,1)S(1)}, f32[64,32,128]{2,1,0:T(8,128)S(1)}, f32[8,8,32,128]{3,2,1,0:T(8,128)S(1)}) custom-call(s32[2,64]{1,0:T(2,128)} %bitcast.21, s32[2,64]{1,0:T(2,128)} %bitcast.22, f32[256,512]{1,0:T(8,128)} %tool_h.1, ...), custom_call_target="tpu_custom_call" | custom-call | tf_op jit(solution)/shard_map/gather_rows/pallas_call | solution.py:339
  27.7 5.4 %contact.1 = f32[8,32,8,128]{3,2,1,0:T(8,128)} custom-call(f32[64,8,128]{2,1,0:T(8,128)S(1)} %get-tuple-element.10.xt, bf16[64,192,64]{2,1,0:T(8,128)(2,1)S(1)} %get-tuple-element.11.lhs, bf16[64,64,192]{2,1,0:T(8,128)(2,1)S(1)} %get-tuple-element.12.vt, f32[64,32,128]{2,1,0:T(8,128)S(1)} %get-tuple-element.13.dw, f32[8,8,32,128]{3,2,1,0:T(8,128)S(1)} %get-tuple-element.14.iw), custom_call_target="tpu_custom_call" | custom-call | tf_op jit(solution)/shard_map/contact/pallas_call | solution.py:358
